TPU v7x, 128 devices: a whole 4x4x4 slice. The times are simulated.
128 devices in a mesh: wide: 16 (over z, y), narrow: 8 (over x, core).
Axes of the slice: x: 4, y: 4, z: 4, core: 2. Of those that a mesh axis runs over, the one named last changes fastest.
Arguments:
- hidden_in: bfloat16 [2048, 2048], P('wide'), may hold values from -6 to 6
- attn_gain: float32 [2048], replicated, may hold values from 0.1 to 1.9
- w_qkv: bfloat16 [2048, 4096], P('wide', 'narrow'), may hold values from -0.125 to 0.125
- q_gain: float32 [128], replicated, may hold values from 0.5 to 10
- k_gain: float32 [128], replicated, may hold values from 0.1 to 1.9
- w_out: bfloat16 [2048, 2048], P('narrow', 'wide'), may hold values from -0.125 to 0.125
- prefix_cache: bfloat16 [2, 64, 4096, 1024], P(None, 'wide', None, 'narrow'), may hold values from -150 to 150
- tail_cache: bfloat16 [2, 1024, 256, 1024], P(None, 'wide', None, 'narrow'), may hold values from -150 to 150
- prompt_lens: int32 [64], replicated, may hold values from 1 to 4096
- tail_lens: int32 [1024], P('wide'), may hold values from 1 to 256
- slot_prompt: int32 [64], replicated, may hold values from 0 to 63, each once
Outputs:
- hidden_out: bfloat16 [2048, 2048], P('wide')
- scores: float32 [2048, 16], P('wide', 'narrow')
- new_cache: bfloat16 [2, 2048, 1024], P(None, 'wide', 'narrow')
Inputs may be any that keep to these rules, and one draw needn't show every extreme that they name: `slot_prompt`: each prompt is held in exactly one slot.
All inputs are finite; a program needn't handle non-finite values.
Results may differ from a plain program's by a relative error of at most 0.007.
Values may be sent and summed in bfloat16 or wider, within the bound.
No kernel may reach another device: no remote copies, remote signals or barrier semaphores. Data moves between devices by JAX's collectives and lax.ppermute only.
A program may use at most 128 MiB of HBM per device.

v0:
```python
import math
import jax
import jax.numpy as jnp
from jax import lax
from jax.sharding import PartitionSpec as P

HEADS = 16
KVH = 8
HD = 128
CONT = 16
NEW = 2
PLEN = 4096
TLEN = 256
epsilon = 1e-06
rope_base = 1000000.0
negative_fill = -1e30


def rms_norm(values, norm_gain):
    mean_square = jnp.mean(values * values, axis=-1, keepdims=True)
    return values * lax.rsqrt(mean_square + epsilon) * norm_gain


def rotate(values, position):
    half_width = values.shape[-1] // 2
    channel = jnp.arange(half_width, dtype=jnp.float32)
    inverse_freq = jnp.exp(channel * (-2.0 / values.shape[-1]) * math.log(rope_base))
    angles = position[..., None] * inverse_freq
    cosine = jnp.cos(angles)
    sines = jnp.sin(angles)
    leading = values[..., :half_width]
    trailing = values[..., half_width:]
    return jnp.concatenate(
        [leading * cosine - trailing * sines, trailing * cosine + leading * sines], axis=-1
    )


def lookup(indices, lookup_table):
    entries = jnp.arange(lookup_table.shape[0], dtype=jnp.int32)
    return jnp.sum(
        jnp.where(indices[:, None] == entries[None, :], lookup_table[None, :], 0), axis=1
    )


def combine_parts(prefix_out, prefix_lse, tail_out, tail_lse):
    highest = jnp.maximum(prefix_lse, tail_lse)
    prefix_share = jnp.exp(prefix_lse - highest)
    tail_share = jnp.exp(tail_lse - highest)
    merged = (prefix_share[..., None] * prefix_out + tail_share[..., None] * tail_out) / (
        prefix_share + tail_share
    )[..., None]
    return (merged.astype(jnp.bfloat16), highest + jnp.log(prefix_share + tail_share))


def body(
    hidden_in,
    attn_gain,
    w_qkv,
    q_gain,
    k_gain,
    w_out,
    prefix_cache,
    tail_cache,
    prompt_lens,
    tail_lens,
    slot_prompt,
):
    group_size = HEADS // KVH
    per_prompt = CONT * NEW
    scaling = HD ** (-0.5)
    wide_index = lax.axis_index("wide")
    rows_dev = hidden_in.shape[0]
    conts_dev = tail_cache.shape[1]
    slot_count = prefix_cache.shape[1]
    groups = prefix_cache.shape[3] // HD
    heads_dev = groups * group_size
    residual = hidden_in.astype(jnp.float32)
    normed = rms_norm(residual, attn_gain).astype(jnp.bfloat16)
    regrouped = lax.all_to_all(normed, "wide", split_axis=1, concat_axis=0, tiled=True)
    projected = lax.psum_scatter(
        jnp.dot(regrouped, w_qkv, preferred_element_type=jnp.float32),
        "wide",
        scatter_dimension=0,
        tiled=True,
    )
    projected = projected.reshape(rows_dev, groups, group_size + 2, HD)
    row_index = wide_index * rows_dev + jnp.arange(rows_dev, dtype=jnp.int32)
    continuation = row_index // NEW
    prompt_index = continuation // CONT
    step_index = row_index % NEW
    local_cont = continuation - wide_index * conts_dev
    position = (
        lookup(prompt_index, prompt_lens) + lookup(local_cont, tail_lens) + step_index
    ).astype(jnp.float32)
    queries = rotate(
        rms_norm(projected[:, :, :group_size], q_gain), position[:, None, None]
    ).astype(jnp.bfloat16)
    new_keys = rotate(rms_norm(projected[:, :, group_size], k_gain), position[:, None]).astype(
        jnp.bfloat16
    )
    new_values = projected[:, :, group_size + 1].astype(jnp.bfloat16)
    everyone = lax.all_gather(queries.reshape(rows_dev, heads_dev * HD), "wide", axis=0, tiled=True)
    global_slot = wide_index * slot_count + jnp.arange(slot_count, dtype=jnp.int32)
    owners = lookup(global_slot, slot_prompt)
    slot_length = lookup(owners, prompt_lens)
    first_row = owners * per_prompt
    chosen = jax.vmap(
        lambda row_begin: lax.dynamic_slice_in_dim(everyone, row_begin, per_prompt, 0)
    )(first_row)
    chosen = chosen.reshape(slot_count, per_prompt, groups, group_size, HD)
    held_keys = prefix_cache[0].reshape(slot_count, PLEN, groups, HD)
    held_values = prefix_cache[1].reshape(slot_count, PLEN, groups, HD)
    prefix_scores = (
        jnp.einsum("srghd,skgd->srghk", chosen, held_keys, preferred_element_type=jnp.float32)
        * scaling
    )
    alive = jnp.arange(PLEN, dtype=jnp.int32)[None, :] < slot_length[:, None]
    prefix_scores = jnp.where(alive[:, None, None, None, :], prefix_scores, negative_fill)
    prefix_max = jnp.max(prefix_scores, axis=-1)
    prefix_weights = jnp.exp(prefix_scores - prefix_max[..., None])
    prefix_total = jnp.sum(prefix_weights, axis=-1)
    prefix_num = jnp.einsum(
        "srghk,skgd->srghd",
        prefix_weights.astype(jnp.bfloat16),
        held_values,
        preferred_element_type=jnp.float32,
    )
    prefix_out = prefix_num / prefix_total[..., None]
    prefix_lse = prefix_max + jnp.log(prefix_total)
    spread_out = jnp.zeros((everyone.shape[0], heads_dev * HD), jnp.float32)
    spread_lse = jnp.zeros((everyone.shape[0], heads_dev), jnp.float32)
    for slot_number in range(slot_count):
        spread_out = lax.dynamic_update_slice_in_dim(
            spread_out,
            prefix_out[slot_number].reshape(per_prompt, heads_dev * HD),
            first_row[slot_number],
            0,
        )
        spread_lse = lax.dynamic_update_slice_in_dim(
            spread_lse,
            prefix_lse[slot_number].reshape(per_prompt, heads_dev),
            first_row[slot_number],
            0,
        )
    mine_out, mine_lse = (
        lax.psum_scatter(spread_out, "wide", scatter_dimension=0, tiled=True),
        lax.psum_scatter(spread_lse, "wide", scatter_dimension=0, tiled=True),
    )
    tail_query = queries.reshape(conts_dev, NEW, groups, group_size, HD)
    tail_keys = tail_cache[0].reshape(conts_dev, TLEN, groups, HD)
    tail_values = tail_cache[1].reshape(conts_dev, TLEN, groups, HD)
    own_keys = new_keys.reshape(conts_dev, NEW, groups, HD)
    own_values = new_values.reshape(conts_dev, NEW, groups, HD)
    cached_scores = (
        jnp.einsum("ctghd,csgd->ctghs", tail_query, tail_keys, preferred_element_type=jnp.float32)
        * scaling
    )
    cached_alive = jnp.arange(TLEN, dtype=jnp.int32)[None, :] < tail_lens[:, None]
    cached_scores = jnp.where(cached_alive[:, None, None, None, :], cached_scores, negative_fill)
    own_scores = (
        jnp.einsum("ctghd,cugd->ctghu", tail_query, own_keys, preferred_element_type=jnp.float32)
        * scaling
    )
    causal = jnp.arange(NEW)[None, :] <= jnp.arange(NEW)[:, None]
    own_scores = jnp.where(causal[None, :, None, None, :], own_scores, negative_fill)
    tail_max = jnp.maximum(jnp.max(cached_scores, axis=-1), jnp.max(own_scores, axis=-1))
    cached_weights = jnp.exp(cached_scores - tail_max[..., None])
    own_weights = jnp.exp(own_scores - tail_max[..., None])
    tail_total = jnp.sum(cached_weights, axis=-1) + jnp.sum(own_weights, axis=-1)
    tail_num = jnp.einsum(
        "ctghs,csgd->ctghd",
        cached_weights.astype(jnp.bfloat16),
        tail_values,
        preferred_element_type=jnp.float32,
    )
    tail_num = tail_num + jnp.einsum(
        "ctghu,cugd->ctghd",
        own_weights.astype(jnp.bfloat16),
        own_values,
        preferred_element_type=jnp.float32,
    )
    tail_out = (tail_num / tail_total[..., None]).reshape(rows_dev, heads_dev, HD)
    tail_lse = (tail_max + jnp.log(tail_total)).reshape(rows_dev, heads_dev)
    attention, scores = combine_parts(
        mine_out.reshape(rows_dev, heads_dev, HD), mine_lse, tail_out, tail_lse
    )
    attention = attention.reshape(rows_dev, heads_dev * HD)
    partial_out = jnp.dot(
        attention,
        lax.all_gather(w_out, "wide", axis=1, tiled=True),
        preferred_element_type=jnp.float32,
    )
    summed = lax.psum(partial_out.astype(jnp.bfloat16), "narrow").astype(jnp.float32)
    hidden_out = (residual + summed).astype(jnp.bfloat16)
    new_cache = jnp.stack(
        [new_keys.reshape(rows_dev, groups * HD), new_values.reshape(rows_dev, groups * HD)]
    )
    return (hidden_out, scores, new_cache)


def solution(mesh):
    in_specs = (
        P("wide", None),
        P(),
        P("wide", "narrow"),
        P(),
        P(),
        P("narrow", "wide"),
        P(None, "wide", None, "narrow"),
        P(None, "wide", None, "narrow"),
        P(),
        P("wide"),
        P(),
    )
    out_specs = (P("wide", None), P("wide", "narrow"), P(None, "wide", "narrow"))
    return jax.shard_map(body, mesh=mesh, in_specs=in_specs, out_specs=out_specs, check_vma=False)
```

profile of v0, /device:TPU:0, one launch (start us, length us, event | category | flops | bytes accessed | tf_op | source)
XLA Modules:
  0.0 435.0 jit_solution(1047986188421033371)
XLA Ops:
  8.5 1.3 copy_bitcast_fusion
  9.8 19.5 %all_to_all.19 = bf16[128,16,128]{2,0,1:T(8,128)(2,1)S(1)} all-to-all(bf16[128,16,128]{2,0,1:T(8,128)(2,1)S(1)} %copy_bitcast_fusion), channel_id=1, replica_groups=mesh['wide'=16,'narrow'=8] {'wide'}, dimensions={1} | all-to-all | bytes 1048576 | tf_op jit(solution)/shard_map/all_to_all | solution.py:79
  29.3 2.6 fusion.99
  32.5 74.9 %reduce-scatter.6.cloned.1.call-done = f32[128,512]{1,0:T(8,128)} async-done(((f32[2048,512]{1,0:T(8,128)}), f32[128,512]{1,0:T(8,128)}) %reduce-scatter.6.cloned.1.call-update) | async-done | bytes 262160 | tf_op jit(solution)/shard_map/reduce_scatter | solution.py:80
  118.9 33.5 %all-gather.3.cloned.1.call-done = bf16[2048,256]{1,0:T(8,128)(2,1)} async-done(((bf16[128,256]{1,0:T(8,128)(2,1)}), bf16[2048,256]{1,0:T(8,128)(2,1)}) %all-gather.3.cloned.1.call-update) | async-done | bytes 1048592 | tf_op jit(solution)/shard_map/all_gather | solution.py:102
  152.4 7.9 %while.1 = (s32[]{:T(128)}, bf16[2048,256]{1,0:T(8,128)(2,1)}, s32[4,2]{0,1:T(2,128)S(1)}, bf16[4,32,256]{2,1,0:T(8,128)(2,1)S(1)}, s32[]{:T(128)}) while((s32[]{:T(128)}, bf16[2048,256]{1,0:T(8,128)(2,1)}, s32[4,2]{0,1:T(2,128)S(1)}, bf16[4,32,256]{2,1,0:T(8,128)(2,1)S(1)}, s32[]{:T(128)}) %tuple.42), condition=%wide.while_cond, body=%wide.while_body.sunk | while | flops 2 | bytes 32865 | solution.py:108
  153.0 1.4 bitcast_dynamic-update-slice_fusion.2
  155.0 1.4 bitcast_dynamic-update-slice_fusion.2
  157.0 1.4 bitcast_dynamic-update-slice_fusion.2
  159.0 1.4 bitcast_dynamic-update-slice_fusion.2
  160.3 3.9 fusion.96
  164.2 1.9 copy-done.1
  167.8 1.4 copy.100
  169.9 4.5 %fusion.45 = f32[4,32,1,2,128]{4,1,3,0,2:T(8,128)S(1)} fusion(bf16[2,4,4096,128]{3,2,1,0:T(8,128)(2,1)} %param.17, f32[4,32,1,2,4096]{4,1,3,0,2:T(8,128)} %copy-done.1, f32[4,32,2]{1,2,0:T(2,128)S(1)} %get-tuple-element.45, f32[4,32,2]{1,2,0:T(2,128)S(1)} %fusion.15), kind=kOutput, calls=%fused_computation.35 | convolution fusion | flops 270565376 | bytes 8521728 | tf_op jit(solution)/shard_map/srghk,skgd->srghd/dot_general | solution.py:122
  176.1 1.3 copy-done.2
  178.5 1.4 fusion.98
  179.9 3.6 fusion.97
  184.6 3.0 fusion.61
  187.7 54.0 %reduce-scatter.10.cloned.1.call-done = f32[128,2]{1,0:T(8,128)} async-done(((f32[2048,2]{1,0:T(8,128)}), f32[128,2]{1,0:T(8,128)}) %reduce-scatter.10.cloned.1.call-update) | async-done | bytes 1040
  243.5 42.9 %all-gather.5.cloned.1.call-done = bf16[256,2048]{1,0:T(8,128)(2,1)} async-done(((bf16[256,128]{1,0:T(8,128)(2,1)}), bf16[256,2048]{1,0:T(8,128)(2,1)}) %all-gather.5.cloned.1.call-update) | async-done | bytes 1048592 | tf_op jit(solution)/shard_map/all_gather | solution.py:190
  286.4 76.9 %reduce-scatter.8.cloned.1.call-done = f32[128,256]{1,0:T(8,128)} async-done(((f32[2048,256]{1,0:T(8,128)}), f32[128,256]{1,0:T(8,128)}) %reduce-scatter.8.cloned.1.call-update) | async-done | bytes 131088 | tf_op jit(solution)/shard_map/reduce_scatter | solution.py:146
  363.8 2.4 convolution_convert_fusion
  367.0 59.2 %all-reduce.3.cloned.1.call-done = bf16[128,2048]{1,0:T(8,128)(2,1)} async-done(((bf16[128,2048]{1,0:T(8,128)(2,1)}), bf16[128,2048]{1,0:T(8,128)(2,1)}) %all-reduce.3.cloned.1.call-update) | async-done | bytes 524304 | tf_op jit(solution)/shard_map/psum | solution.py:193
  426.2 2.0 fusion.54
  (106 shorter events, 17.3 us)
Async XLA Ops:
  7.2 22.1 %copy-start = (bf16[128,512]{1,0:T(8,128)(2,1)S(1)}, bf16[128,512]{1,0:T(8,128)(2,1)}, u32[]{:S(2)}) copy-start(bf16[128,512]{1,0:T(8,128)(2,1)} %param.13) | copy-start | bytes 393220
  7.2 100.2 %reduce-scatter.6.cloned.1.call-start = ((), (), s32[]{:S(2)}) async-start(), calls=%async_computation.4 | async-start | bytes 4456448 | tf_op jit(solution)/shard_map/reduce_scatter | solution.py:80
  29.2 2.7 copy-start.6
  29.3 2.8 copy-start.8
  29.3 79.4 %copy-start.4 = (f32[128]{0:T(128)S(1)}, f32[128]{0:T(128)}, u32[]{:S(2)}) copy-start(f32[128]{0:T(128)} %param.14) | copy-start | bytes 1540
  31.9 78.3 %copy-start.7 = (s32[64]{0:T(128)S(1)}, s32[64]{0:T(128)}, u32[]{:S(2)}) copy-start(s32[64]{0:T(128)} %param.21) | copy-start | bytes 772
  31.9 120.6 %all-gather.3.cloned.1.call-start = ((), (), s32[]{:S(2)}) async-start(), calls=%async_computation.5 | async-start | bytes 1114112 | tf_op jit(solution)/shard_map/all_gather | solution.py:102
  110.1 131.6 %reduce-scatter.10.cloned.1.call-start = ((), (), s32[]{:S(2)}) async-start(), calls=%async_computation.9 | async-start | bytes 1114112
  164.2 1.9 copy-start.1
  169.2 117.1 %all-gather.5.cloned.1.call-start = ((), (), s32[]{:S(2)}) async-start(), calls=%async_computation.7 | async-start | bytes 1114112 | tf_op jit(solution)/shard_map/all_gather | solution.py:190
  169.8 193.4 %reduce-scatter.8.cloned.1.call-start = ((), (), s32[]{:S(2)}) async-start(), calls=%async_computation.6 | async-start | bytes 2228224 | tf_op jit(solution)/shard_map/reduce_scatter | solution.py:146
  174.4 3.7 copy-start.5
  176.1 1.4 copy-start.2
  177.5 248.7 %all-reduce.3.cloned.1.call-start = ((), (), s32[]{:S(2)}) async-start(), calls=%async_computation.8 | async-start | bytes 1048576 | tf_op jit(solution)/shard_map/psum | solution.py:193
  184.6 241.6 %copy-start.3 = (bf16[128,2048]{1,0:T(8,128)(2,1)S(1)}, bf16[128,2048]{1,0:T(8,128)(2,1)}, u32[]{:S(2)}) copy-start(bf16[128,2048]{1,0:T(8,128)(2,1)} %param.11) | copy-start | bytes 1572868
Sparse Core Ops, SparseCore 0:
  32.0 75.3 reduce-scatter.5
  110.4 42.0 all-gather.2
  169.4 72.2 reduce-scatter.9
  243.6 42.6 all-gather.4
  289.5 73.7 reduce-scatter.7
  366.4 59.7 all-reduce.2
where the time goes:
time: 436 us; the launch traced here: 435 us
  waiting for transfers between devices  342 us (78%)
  between operations  22.1 us (5%)
  matrix products  21.7 us (5%)
  local copies, waits for them, and re-layouts  19.5 us (4%)
  blocking collectives  19.5 us (4%)
  other arithmetic  9.84 us (2%)
    reduce_scatter x1, waiting for transfers between devices, body(): lax.psum_scatter(spread_out, 'wide', scatter_dimension=0, tiled=True)  76.9 us
    reduce_scatter x1, waiting for transfers between devices, body(): lax.psum_scatter(jnp.dot(regrouped, w_qkv, preferred_element_type=jnp.flo...  74.9 us
    psum x1, waiting for transfers between devices, body(): lax.psum(partial_out.astype(jnp.bfloat16), 'narrow').astype(jnp.float32)  59.2 us
    unnamed x7, waiting for transfers between devices  54.6 us
    all_gather x1, waiting for transfers between devices, body(): lax.all_gather(w_out, 'wide', axis=1, tiled=True)  42.9 us
    all_gather x1, waiting for transfers between devices, body(): lax.all_gather(queries.reshape(rows_dev, heads_dev * HD), 'wide', axis=0,...  33.5 us
    all_to_all x1, blocking collectives, body(): lax.all_to_all(normed, 'wide', split_axis=1, concat_axis=0, tiled=True)  19.5 us
  transfers between devices with their start and end apart: 6, of which 6 were waited for; matrix products, arithmetic and copies ran while one was open for 5% of the time, Pallas kernels for 0%

commit v1 on v0

--- a/solution.py
+++ b/solution.py
@@ -14,6 +14,28 @@
 epsilon = 1e-06
 rope_base = 1000000.0
 negative_fill = -1e30
+
+
+def in_order(parts, dim):
+    shape = list(parts.shape[1:])
+    shape[dim] *= parts.shape[0]
+    return jnp.moveaxis(parts, 0, dim).reshape(shape)
+
+
+def ring_gather(value, axis, dim):
+    size = lax.axis_size(axis)
+    pairs = [(i, (i + 1) % size) for i in range(size)]
+    back = [(b, a) for a, b in pairs]
+    lower, upper = ([], [])
+    for step in range(size - 1):
+        if step % 2 == 0:
+            lower.append(lax.ppermute(lower[-1] if lower else value, axis, pairs))
+        else:
+            upper.append(lax.ppermute(upper[-1] if upper else value, axis, back))
+    parts = jnp.stack([*lower[::-1], value, *upper])
+    shift = lax.axis_index(axis) - len(lower)
+    parts = parts[(jnp.arange(size) - shift) % size]
+    return in_order(parts, dim)
 
 
 def rms_norm(values, norm_gain):
@@ -186,9 +208,7 @@
     )
     attention = attention.reshape(rows_dev, heads_dev * HD)
     partial_out = jnp.dot(
-        attention,
-        lax.all_gather(w_out, "wide", axis=1, tiled=True),
-        preferred_element_type=jnp.float32,
+        attention, ring_gather(w_out, "wide", 1), preferred_element_type=jnp.float32
     )
     summed = lax.psum(partial_out.astype(jnp.bfloat16), "narrow").astype(jnp.float32)
     hidden_out = (residual + summed).astype(jnp.bfloat16)

time: 436 us -> 393 us (0.901)
  waiting for transfers between devices: 342 us -> 249 us
  starting transfers between devices: 0.42 us -> 39.3 us
  local copies, waits for them, and re-layouts: 19.5 us -> 28 us
    reduce_scatter x1, waiting for transfers between devices: 74.9 us -> 5.9 us  [body(): lax.psum_scatter(jnp.dot(regrouped, w_qkv, preferred_element_type=jnp.flo...]
    all_gather x1 -> x0, waiting for transfers between devices: 42.9 us -> none  [body(): lax.all_gather(w_out, 'wide', axis=1, tiled=True)]
    ppermute x0 -> x15, starting transfers between devices: none -> 38.9 us  [the longest x7 38.3 us: ring_gather(): upper.append(lax.ppermute(upper[-1] if upper else value, axis, back))]
    ppermute x0 -> x15, waiting for transfers between devices: none -> 21.1 us  [the longest x8 16.4 us: ring_gather(): lower.append(lax.ppermute(lower[-1] if lower else value, axis, pairs))]
    all_gather x1, waiting for transfers between devices: 33.5 us -> 41.8 us  [body(): lax.all_gather(queries.reshape(rows_dev, heads_dev * HD), 'wide', axis=0,...]
    unnamed x7 -> x6, waiting for transfers between devices: 54.6 us -> 46.5 us
    unnamed x25 -> x52, local copies, waits for them, and re-layouts: 6.26 us -> 10.3 us
  transfers between devices with their start and end apart: 6 -> 20, of which waited for: 6 -> 12; matrix products, arithmetic and copies ran while one was open for 5% -> 13% of each run, Pallas kernels for 0% -> 0%
where the time goes in v1:
time: 393 us; the launch traced here: 392 us
  waiting for transfers between devices  249 us (63%)
  starting transfers between devices  39.3 us (10%)
  local copies, waits for them, and re-layouts  28 us (7%)
  between operations  22.1 us (6%)
  matrix products  21.2 us (5%)
  blocking collectives  19.5 us (5%)
  other arithmetic  12.3 us (3%)
    reduce_scatter x1, waiting for transfers between devices, body(): lax.psum_scatter(spread_out, 'wide', scatter_dimension=0, tiled=True)  75.1 us
    psum x1, waiting for transfers between devices, body(): lax.psum(partial_out.astype(jnp.bfloat16), 'narrow').astype(jnp.float32)  59.1 us
    unnamed x6, waiting for transfers between devices  46.5 us
    all_gather x1, waiting for transfers between devices, body(): lax.all_gather(queries.reshape(rows_dev, heads_dev * HD), 'wide', axis=0,...  41.8 us
    ppermute x7, starting transfers between devices, ring_gather(): upper.append(lax.ppermute(upper[-1] if upper else value, axis, back))  38.3 us
    all_to_all x1, blocking collectives, body(): lax.all_to_all(normed, 'wide', split_axis=1, concat_axis=0, tiled=True)  19.5 us
    ppermute x8, waiting for transfers between devices, ring_gather(): lower.append(lax.ppermute(lower[-1] if lower else value, axis, pairs))  16.4 us
    unnamed x52, local copies, waits for them, and re-layouts  10.3 us
  transfers between devices with their start and end apart: 20, of which 12 were waited for; matrix products, arithmetic and copies ran while one was open for 13% of the time, Pallas kernels for 0%

profile of v1, /device:TPU:0, one launch (start us, length us, event | category | flops | bytes accessed | tf_op | source)
XLA Modules:
  0.0 391.9 jit_solution(2683944788350190424)
XLA Ops:
  9.8 19.5 %all_to_all.19 = bf16[128,16,128]{2,0,1:T(8,128)(2,1)S(1)} all-to-all(bf16[128,16,128]{2,0,1:T(8,128)(2,1)S(1)} %copy_bitcast_fusion), channel_id=1, replica_groups=mesh['wide'=16,'narrow'=8] {'wide'}, dimensions={1} | all-to-all | bytes 1048576 | tf_op jit(solution)/shard_map/all_to_all | solution.py:101
  29.3 2.6 fusion.101
  32.6 4.8 %collective-permute-start.8 = (bf16[256,128]{1,0:T(8,128)(2,1)S(1)}, bf16[256,128]{1,0:T(8,128)(2,1)S(1)}, u32[]{:S(2)}, u32[]{:S(2)}) collective-permute-start(bf16[256,128]{1,0:T(8,128)(2,1)S(1)} %copy-done.5), channel_id=1, source_target_pairs={{8,0},{16,8},{24,16},{32,24},{40,32},{48,40},{56,48},{64,56},{72,6... | collective-permute-start | bytes 196616 | tf_op jit(solution)/shard_map/ppermute | solution.py:34
  39.7 8.2 %collective-permute-done.1 = bf16[256,128]{1,0:T(8,128)(2,1)S(1)} collective-permute-done((bf16[256,128]{1,0:T(8,128)(2,1)S(1)}, bf16[256,128]{1,0:T(8,128)(2,1)S(1)}, u32[]{:S(2)}, u32[]{:S(2)}) %collective-permute-start.1) | collective-permute-done | bytes 65568 | tf_op jit(solution)/shard_map/ppermute | solution.py:32
  47.9 5.3 %collective-permute-start.9 = (bf16[256,128]{1,0:T(8,128)(2,1)S(1)}, bf16[256,128]{1,0:T(8,128)(2,1)S(1)}, u32[]{:S(2)}, u32[]{:S(2)}) collective-permute-start(bf16[256,128]{1,0:T(8,128)(2,1)S(1)} %collective-permute-done.8), channel_id=1, source_target_pairs={{8,0},{16,8},{24,16},{32,24},{40,32},{48,40},{56,48},{64,56},{72,6... | collective-permute-start | bytes 196616 | tf_op jit(solution)/shard_map/ppermute | solution.py:34
  53.3 3.1 collective-permute-done.2
  56.4 5.4 %collective-permute-start.10 = (bf16[256,128]{1,0:T(8,128)(2,1)S(1)}, bf16[256,128]{1,0:T(8,128)(2,1)S(1)}, u32[]{:S(2)}, u32[]{:S(2)}) collective-permute-start(bf16[256,128]{1,0:T(8,128)(2,1)S(1)} %collective-permute-done.9), channel_id=1, source_target_pairs={{8,0},{16,8},{24,16},{32,24},{40,32},{48,40},{56,48},{64,56},{72,6... | collective-permute-start | bytes 196616 | tf_op jit(solution)/shard_map/ppermute | solution.py:34
  61.8 3.9 collective-permute-done.3
  74.2 5.4 %collective-permute-start.11 = (bf16[256,128]{1,0:T(8,128)(2,1)S(1)}, bf16[256,128]{1,0:T(8,128)(2,1)S(1)}, u32[]{:S(2)}, u32[]{:S(2)}) collective-permute-start(bf16[256,128]{1,0:T(8,128)(2,1)S(1)} %collective-permute-done.10), channel_id=1, source_target_pairs={{8,0},{16,8},{24,16},{32,24},{40,32},{48,40},{56,48},{64,56},{72,6... | collective-permute-start | bytes 196616 | tf_op jit(solution)/shard_map/ppermute | solution.py:34
  81.7 5.8 %collective-permute-start.12 = (bf16[256,128]{1,0:T(8,128)(2,1)S(1)}, bf16[256,128]{1,0:T(8,128)(2,1)S(1)}, u32[]{:S(2)}, u32[]{:S(2)}) collective-permute-start(bf16[256,128]{1,0:T(8,128)(2,1)S(1)} %collective-permute-done.11), channel_id=1, source_target_pairs={{8,0},{16,8},{24,16},{32,24},{40,32},{48,40},{56,48},{64,56},{72,6... | collective-permute-start | bytes 196616 | tf_op jit(solution)/shard_map/ppermute | solution.py:34
  89.4 5.7 %collective-permute-start.13 = (bf16[256,128]{1,0:T(8,128)(2,1)S(1)}, bf16[256,128]{1,0:T(8,128)(2,1)}, u32[]{:S(2)}, u32[]{:S(2)}) collective-permute-start(bf16[256,128]{1,0:T(8,128)(2,1)S(1)} %collective-permute-done.12), channel_id=1, source_target_pairs={{8,0},{16,8},{24,16},{32,24},{40,32},{48,40},{56,48},{64,56},{72,6... | collective-permute-start | bytes 196616 | tf_op jit(solution)/shard_map/ppermute | solution.py:34
  97.0 5.9 %collective-permute-start.14 = (bf16[256,128]{1,0:T(8,128)(2,1)}, bf16[256,128]{1,0:T(8,128)(2,1)}, u32[]{:S(2)}, u32[]{:S(2)}) collective-permute-start(bf16[256,128]{1,0:T(8,128)(2,1)} %collective-permute-done.13), channel_id=1, source_target_pairs={{8,0},{16,8},{24,16},{32,24},{40,32},{48,40},{56,48},{64,56},{72,6... | collective-permute-start | bytes 196616 | tf_op jit(solution)/shard_map/ppermute | solution.py:34
  102.9 5.9 %reduce-scatter.6.cloned.1.call-done = f32[128,512]{1,0:T(8,128)} async-done(((f32[2048,512]{1,0:T(8,128)}), f32[128,512]{1,0:T(8,128)}) %reduce-scatter.6.cloned.1.call-update) | async-done | bytes 262160 | tf_op jit(solution)/shard_map/reduce_scatter | solution.py:102
  111.9 41.8 %all-gather.2.cloned.1.call-done = bf16[2048,256]{1,0:T(8,128)(2,1)} async-done(((bf16[128,256]{1,0:T(8,128)(2,1)}), bf16[2048,256]{1,0:T(8,128)(2,1)}) %all-gather.2.cloned.1.call-update) | async-done | bytes 1048592 | tf_op jit(solution)/shard_map/all_gather | solution.py:124
  153.7 7.5 %while.1 = (s32[]{:T(128)}, bf16[2048,256]{1,0:T(8,128)(2,1)}, s32[4,2]{0,1:T(2,128)S(1)}, bf16[4,32,256]{2,1,0:T(8,128)(2,1)S(1)}, s32[]{:T(128)}) while((s32[]{:T(128)}, bf16[2048,256]{1,0:T(8,128)(2,1)}, s32[4,2]{0,1:T(2,128)S(1)}, bf16[4,32,256]{2,1,0:T(8,128)(2,1)S(1)}, s32[]{:T(128)}) %tuple.42), condition=%wide.while_cond, body=%wide.while_body.sunk | while | flops 2 | bytes 32865 | solution.py:130
  161.2 3.8 fusion.98
  165.8 3.3 fusion.45
  187.3 2.3 fusion.100
  189.6 3.6 fusion.99
  194.4 3.0 fusion.61
  197.4 46.5 %reduce-scatter.10.cloned.1.call-done = f32[128,2]{1,0:T(8,128)} async-done(((f32[2048,2]{1,0:T(8,128)}), f32[128,2]{1,0:T(8,128)}) %reduce-scatter.10.cloned.1.call-update) | async-done | bytes 1040
  245.7 75.1 %reduce-scatter.8.cloned.1.call-done = f32[128,256]{1,0:T(8,128)} async-done(((f32[2048,256]{1,0:T(8,128)}), f32[128,256]{1,0:T(8,128)}) %reduce-scatter.8.cloned.1.call-update) | async-done | bytes 131088 | tf_op jit(solution)/shard_map/reduce_scatter | solution.py:168
  321.4 2.2 convolution_convert_fusion
  324.3 59.1 %all-reduce.3.cloned.1.call-done = bf16[128,2048]{1,0:T(8,128)(2,1)} async-done(((bf16[128,2048]{1,0:T(8,128)(2,1)}), bf16[128,2048]{1,0:T(8,128)(2,1)}) %all-reduce.3.cloned.1.call-update) | async-done | bytes 524304 | tf_op jit(solution)/shard_map/psum | solution.py:213
  (165 shorter events, 47.7 us)
Async XLA Ops:
  7.2 22.1 %copy-start = (bf16[128,512]{1,0:T(8,128)(2,1)S(1)}, bf16[128,512]{1,0:T(8,128)(2,1)}, u32[]{:S(2)}) copy-start(bf16[128,512]{1,0:T(8,128)(2,1)} %param.13) | copy-start | bytes 393220
  7.2 101.6 %reduce-scatter.6.cloned.1.call-start = ((), (), s32[]{:S(2)}) async-start(), calls=%async_computation.4 | async-start | bytes 4456448 | tf_op jit(solution)/shard_map/reduce_scatter | solution.py:102
  29.3 80.8 %copy-start.11 = (f32[128]{0:T(128)S(1)}, f32[128]{0:T(128)}, u32[]{:S(2)}) copy-start(f32[128]{0:T(128)} %param.14) | copy-start | bytes 1540
  31.9 121.8 %all-gather.2.cloned.1.call-start = ((), (), s32[]{:S(2)}) async-start(), calls=%async_computation.5 | async-start | bytes 1114112 | tf_op jit(solution)/shard_map/all_gather | solution.py:124
  32.0 7.7 %collective-permute-start = (bf16[256,128]{1,0:T(8,128)(2,1)S(1)}, bf16[256,128]{1,0:T(8,128)(2,1)S(1)}, u32[]{:S(2)}, u32[]{:S(2)}) collective-permute-start(bf16[256,128]{1,0:T(8,128)(2,1)S(1)} %copy-done.5), channel_id=1, source_target_pairs={{0,8},{8,16},{16,24},{24,32},{32,40},{40,48},{48,56},{56,64},{64,7... | collective-permute-start | bytes 196616 | tf_op jit(solution)/shard_map/ppermute | solution.py:32
  32.6 15.3 %collective-permute-start.8 = (bf16[256,128]{1,0:T(8,128)(2,1)S(1)}, bf16[256,128]{1,0:T(8,128)(2,1)S(1)}, u32[]{:S(2)}, u32[]{:S(2)}) collective-permute-start(bf16[256,128]{1,0:T(8,128)(2,1)S(1)} %copy-done.5), channel_id=1, source_target_pairs={{8,0},{16,8},{24,16},{32,24},{40,32},{48,40},{56,48},{64,56},{72,6... | collective-permute-start | bytes 196616 | tf_op jit(solution)/shard_map/ppermute | solution.py:34
  39.6 8.3 %collective-permute-start.1 = (bf16[256,128]{1,0:T(8,128)(2,1)S(1)}, bf16[256,128]{1,0:T(8,128)(2,1)S(1)}, u32[]{:S(2)}, u32[]{:S(2)}) collective-permute-start(bf16[256,128]{1,0:T(8,128)(2,1)S(1)} %collective-permute-done), channel_id=1, source_target_pairs={{0,8},{8,16},{16,24},{24,32},{32,40},{40,48},{48,56},{56,64},{64,7... | collective-permute-start | bytes 196616 | tf_op jit(solution)/shard_map/ppermute | solution.py:32
  47.9 8.4 %collective-permute-start.2 = (bf16[256,128]{1,0:T(8,128)(2,1)S(1)}, bf16[256,128]{1,0:T(8,128)(2,1)S(1)}, u32[]{:S(2)}, u32[]{:S(2)}) collective-permute-start(bf16[256,128]{1,0:T(8,128)(2,1)S(1)} %collective-permute-done.1), channel_id=1, source_target_pairs={{0,8},{8,16},{16,24},{24,32},{32,40},{40,48},{48,56},{56,64},{64,7... | collective-permute-start | bytes 196616 | tf_op jit(solution)/shard_map/ppermute | solution.py:32
  47.9 8.5 %collective-permute-start.9 = (bf16[256,128]{1,0:T(8,128)(2,1)S(1)}, bf16[256,128]{1,0:T(8,128)(2,1)S(1)}, u32[]{:S(2)}, u32[]{:S(2)}) collective-permute-start(bf16[256,128]{1,0:T(8,128)(2,1)S(1)} %collective-permute-done.8), channel_id=1, source_target_pairs={{8,0},{16,8},{24,16},{32,24},{40,32},{48,40},{56,48},{64,56},{72,6... | collective-permute-start | bytes 196616 | tf_op jit(solution)/shard_map/ppermute | solution.py:34
  56.4 9.3 %collective-permute-start.3 = (bf16[256,128]{1,0:T(8,128)(2,1)S(1)}, bf16[256,128]{1,0:T(8,128)(2,1)S(1)}, u32[]{:S(2)}, u32[]{:S(2)}) collective-permute-start(bf16[256,128]{1,0:T(8,128)(2,1)S(1)} %collective-permute-done.2), channel_id=1, source_target_pairs={{0,8},{8,16},{16,24},{24,32},{32,40},{40,48},{48,56},{56,64},{64,7... | collective-permute-start | bytes 196616 | tf_op jit(solution)/shard_map/ppermute | solution.py:32
  56.4 17.7 %collective-permute-start.10 = (bf16[256,128]{1,0:T(8,128)(2,1)S(1)}, bf16[256,128]{1,0:T(8,128)(2,1)S(1)}, u32[]{:S(2)}, u32[]{:S(2)}) collective-permute-start(bf16[256,128]{1,0:T(8,128)(2,1)S(1)} %collective-permute-done.9), channel_id=1, source_target_pairs={{8,0},{16,8},{24,16},{32,24},{40,32},{48,40},{56,48},{64,56},{72,6... | collective-permute-start | bytes 196616 | tf_op jit(solution)/shard_map/ppermute | solution.py:34
  65.7 13.9 %collective-permute-start.4 = (bf16[256,128]{1,0:T(8,128)(2,1)S(1)}, bf16[256,128]{1,0:T(8,128)(2,1)S(1)}, u32[]{:S(2)}, u32[]{:S(2)}) collective-permute-start(bf16[256,128]{1,0:T(8,128)(2,1)S(1)} %collective-permute-done.3), channel_id=1, source_target_pairs={{0,8},{8,16},{16,24},{24,32},{32,40},{40,48},{48,56},{56,64},{64,7... | collective-permute-start | bytes 196616 | tf_op jit(solution)/shard_map/ppermute | solution.py:32
  74.1 28.7 %copy-start.6 = (bf16[256,128]{1,0:T(8,128)(2,1)}, bf16[256,128]{1,0:T(8,128)(2,1)S(1)}, u32[]{:S(2)}) copy-start(bf16[256,128]{1,0:T(8,128)(2,1)S(1)} %collective-permute-done.10) | copy-start | bytes 196612
  74.2 7.5 %collective-permute-start.11 = (bf16[256,128]{1,0:T(8,128)(2,1)S(1)}, bf16[256,128]{1,0:T(8,128)(2,1)S(1)}, u32[]{:S(2)}, u32[]{:S(2)}) collective-permute-start(bf16[256,128]{1,0:T(8,128)(2,1)S(1)} %collective-permute-done.10), channel_id=1, source_target_pairs={{8,0},{16,8},{24,16},{32,24},{40,32},{48,40},{56,48},{64,56},{72,6... | collective-permute-start | bytes 196616 | tf_op jit(solution)/shard_map/ppermute | solution.py:34
  79.6 7.9 %collective-permute-start.5 = (bf16[256,128]{1,0:T(8,128)(2,1)S(1)}, bf16[256,128]{1,0:T(8,128)(2,1)S(1)}, u32[]{:S(2)}, u32[]{:S(2)}) collective-permute-start(bf16[256,128]{1,0:T(8,128)(2,1)S(1)} %collective-permute-done.4), channel_id=1, source_target_pairs={{0,8},{8,16},{16,24},{24,32},{32,40},{40,48},{48,56},{56,64},{64,7... | collective-permute-start | bytes 196616 | tf_op jit(solution)/shard_map/ppermute | solution.py:32
  81.7 7.7 %collective-permute-start.12 = (bf16[256,128]{1,0:T(8,128)(2,1)S(1)}, bf16[256,128]{1,0:T(8,128)(2,1)S(1)}, u32[]{:S(2)}, u32[]{:S(2)}) collective-permute-start(bf16[256,128]{1,0:T(8,128)(2,1)S(1)} %collective-permute-done.11), channel_id=1, source_target_pairs={{8,0},{16,8},{24,16},{32,24},{40,32},{48,40},{56,48},{64,56},{72,6... | collective-permute-start | bytes 196616 | tf_op jit(solution)/shard_map/ppermute | solution.py:34
  87.5 7.6 %collective-permute-start.6 = (bf16[256,128]{1,0:T(8,128)(2,1)S(1)}, bf16[256,128]{1,0:T(8,128)(2,1)S(1)}, u32[]{:S(2)}, u32[]{:S(2)}) collective-permute-start(bf16[256,128]{1,0:T(8,128)(2,1)S(1)} %collective-permute-done.5), channel_id=1, source_target_pairs={{0,8},{8,16},{16,24},{24,32},{32,40},{40,48},{48,56},{56,64},{64,7... | collective-permute-start | bytes 196616 | tf_op jit(solution)/shard_map/ppermute | solution.py:32
  89.4 7.6 %collective-permute-start.13 = (bf16[256,128]{1,0:T(8,128)(2,1)S(1)}, bf16[256,128]{1,0:T(8,128)(2,1)}, u32[]{:S(2)}, u32[]{:S(2)}) collective-permute-start(bf16[256,128]{1,0:T(8,128)(2,1)S(1)} %collective-permute-done.12), channel_id=1, source_target_pairs={{8,0},{16,8},{24,16},{32,24},{40,32},{48,40},{56,48},{64,56},{72,6... | collective-permute-start | bytes 196616 | tf_op jit(solution)/shard_map/ppermute | solution.py:34
  95.1 7.8 %collective-permute-start.7 = (bf16[256,128]{1,0:T(8,128)(2,1)S(1)}, bf16[256,128]{1,0:T(8,128)(2,1)S(1)}, u32[]{:S(2)}, u32[]{:S(2)}) collective-permute-start(bf16[256,128]{1,0:T(8,128)(2,1)S(1)} %collective-permute-done.6), channel_id=1, source_target_pairs={{0,8},{8,16},{16,24},{24,32},{32,40},{40,48},{48,56},{56,64},{64,7... | collective-permute-start | bytes 196616 | tf_op jit(solution)/shard_map/ppermute | solution.py:32
  97.0 86.0 %collective-permute-start.14 = (bf16[256,128]{1,0:T(8,128)(2,1)}, bf16[256,128]{1,0:T(8,128)(2,1)}, u32[]{:S(2)}, u32[]{:S(2)}) collective-permute-start(bf16[256,128]{1,0:T(8,128)(2,1)} %collective-permute-done.13), channel_id=1, source_target_pairs={{8,0},{16,8},{24,16},{32,24},{40,32},{48,40},{56,48},{64,56},{72,6... | collective-permute-start | bytes 196616 | tf_op jit(solution)/shard_map/ppermute | solution.py:34
  111.5 132.4 %reduce-scatter.10.cloned.1.call-start = ((), (), s32[]{:S(2)}) async-start(), calls=%async_computation.8 | async-start | bytes 1114112
  171.4 149.4 %reduce-scatter.8.cloned.1.call-start = ((), (), s32[]{:S(2)}) async-start(), calls=%async_computation.6 | async-start | bytes 2228224 | tf_op jit(solution)/shard_map/reduce_scatter | solution.py:168
  179.6 203.9 %all-reduce.3.cloned.1.call-start = ((), (), s32[]{:S(2)}) async-start(), calls=%async_computation.7 | async-start | bytes 1048576 | tf_op jit(solution)/shard_map/psum | solution.py:213
  194.4 189.1 %copy-start.2 = (bf16[128,2048]{1,0:T(8,128)(2,1)S(1)}, bf16[128,2048]{1,0:T(8,128)(2,1)}, u32[]{:S(2)}) copy-start(bf16[128,2048]{1,0:T(8,128)(2,1)} %param.11) | copy-start | bytes 1572868
  (11 other events, 102.9 us)
Sparse Core Ops, SparseCore 0:
  32.1 76.7 reduce-scatter.5
  111.6 42.0 all-gather.1
  171.5 72.3 reduce-scatter.9
  247.0 73.7 reduce-scatter.7
  323.7 59.6 all-reduce.2
